TPU v7x, 32 devices: a whole 2x2x4 slice. The times are simulated.
32 devices in a mesh: rows: 8 (over y, x, core), cols: 4 (over z).
Axes of the slice: x: 2, y: 2, z: 4, core: 2. Of those that a mesh axis runs over, the one named last changes fastest.
Arguments:
- coords: int32 [8, 16384], P(None, ('rows', 'cols')), may hold values from 0 to 4095
- probes: float32 [64, 16384], P(None, ('rows', 'cols')), may hold values from -6 to 6
- lengthscales: float32 [8], replicated, may hold values from 0.15 to 0.25
- amplitude: float32 [1], replicated, may hold values from 0.1 to 0.3
- landmarks: float32 [14, 8, 128], replicated, may hold values from 0 to 1
- coupling: float32 [128, 128], replicated, may hold values from -0.5 to 0.5
Outputs:
- products: float32 [2, 64, 16384], P(None, None, ('rows', 'cols'))
All inputs are finite; a program needn't handle non-finite values.
Results may differ from a plain program's by a relative error of at most 0.0025.
Values may be sent and summed in bfloat16 or wider, within the bound.
A program may use at most 64 MiB of HBM per device.

v0:
```python
import jax
import jax.numpy as jnp
from jax import lax
from jax.sharding import PartitionSpec as P


def swapped(array, axis, apart):
    return lax.ppermute(array, axis, [(i, i ^ 1 << apart) for i in range(lax.axis_size(axis))])


def pair_squares(left_points, right_points):
    squared = jnp.zeros((left_points.shape[1], right_points.shape[1]), jnp.float32)
    for component in range(left_points.shape[0]):
        offset = left_points[component][:, None] - right_points[component][None, :]
        squared = squared + offset * offset
    return squared


def on_device(coords, probes, lengthscales, amplitude, landmarks, coupling):
    highest = lax.Precision.HIGHEST
    inverse_scale = 1.0 / lengthscales
    scaled = coords.astype(jnp.float32) * (1.0 / 4096.0) * inverse_scale[:, None]
    strength = amplitude[0]
    signs_half = probes.astype(jnp.bfloat16)
    width = coords.shape[1]
    groups = lax.axis_size("cols")
    rows_index = lax.axis_index("rows")
    levels = lax.axis_size("rows").bit_length() - 1
    leaf_points = lax.all_gather(scaled, "cols", axis=1, tiled=True)
    leaf_signs = lax.all_gather(signs_half, "cols", axis=1, tiled=True)
    accumulated = jnp.zeros((2, probes.shape[0], width), jnp.float32)
    for row_block in range(groups):
        block_points = leaf_points[:, row_block * width : (row_block + 1) * width]
        block_signs = leaf_signs[:, row_block * width : (row_block + 1) * width]
        squared = pair_squares(block_points, scaled)
        kernel = strength * jnp.exp(-0.5 * squared)
        kernel_half = kernel.astype(jnp.bfloat16)
        slope_half = (kernel * squared).astype(jnp.bfloat16)
        accumulated = accumulated + jnp.stack(
            [
                jnp.dot(block_signs, kernel_half, preferred_element_type=jnp.float32),
                jnp.dot(block_signs, slope_half, preferred_element_type=jnp.float32),
            ]
        )
    result = accumulated
    factor_list = []
    dfactor_list = []
    for level in range(levels):
        depth = levels - level
        node = jnp.right_shift(rows_index, level)
        chosen = lax.dynamic_index_in_dim(landmarks, 2**depth - 2 + node, 0, keepdims=False)
        squared = pair_squares(scaled, chosen * inverse_scale[:, None])
        factor = strength * jnp.exp(-0.5 * squared)
        factor_list.append(factor)
        dfactor_list.append(factor * squared)
    factor_stack = jnp.stack(factor_list)
    dfactor_stack = jnp.stack(dfactor_list)
    own_project = jnp.einsum("pn,lnr->lpr", probes, factor_stack, precision=highest)
    own_dproject = jnp.einsum("pn,lnr->lpr", probes, dfactor_stack, precision=highest)
    projections = lax.psum(jnp.stack([own_project, own_dproject], axis=1), "cols")
    siblings = []
    pending = projections
    for level in range(levels):
        partner = swapped(pending[level:], "rows", level)
        siblings.append(partner[0])
        pending = pending.at[level + 1 :].add(partner[1:])
    for level in range(levels):
        sibling_sums = siblings[level]
        is_left = jnp.right_shift(rows_index, level) & 1 == 0
        core = jnp.where(is_left, coupling.T, coupling)
        first = jnp.dot(sibling_sums[0], core, precision=highest)
        second = jnp.dot(sibling_sums[1], core, precision=highest)
        value = jnp.dot(first, factor_stack[level].T, precision=highest)
        slope = jnp.dot(first, dfactor_stack[level].T, precision=highest) + jnp.dot(
            second, factor_stack[level].T, precision=highest
        )
        result = result + jnp.stack([value, slope])
    return result


def solution(mesh):
    in_specs = (P(None, ("rows", "cols")), P(None, ("rows", "cols")), P(), P(), P(), P())
    out_specs = P(None, None, ("rows", "cols"))
    return jax.shard_map(
        on_device, mesh=mesh, in_specs=in_specs, out_specs=out_specs, check_vma=False
    )
```

profile of v0, /device:TPU:0, one launch (start us, length us, event | category | flops | bytes accessed | tf_op | source)
XLA Modules:
  0.0 75.2 jit_solution(17061877505005976449)
XLA Ops:
  6.5 0.7 copy-done.4
  7.2 0.0 copy-done.3
  7.3 0.1 convert_multiply_fusion
  8.0 0.8 %bitcast_multiply_fusion.2 = (f32[8,128]{1,0:T(8,128)S(1)}, f32[8,128]{1,0:T(8,128)S(1)}, f32[8,128]{1,0:T(8,128)S(1)}) fusion(f32[14,8,128]{2,1,0:T(8,128)} %param.14, s32[]{:T(128)S(6)} %select_n.30, f32[8]{0:T(128)S(1)} %get-tuple-element.30, s32[]{:T(128)S(6)} %select_n.32, s32[]{:T(128)S(6)} %select_n.31), kind=kLoop, calls=%fused_computation.137 | loop fusion | flops 3072 | bytes 24620 | tf_op jit(solution)/shard_map/mul | solution.py:52
  8.8 0.6 exponential_multiply_fusion.17
  9.4 0.6 exponential_multiply_fusion.16
  10.1 0.0 copy-start.1
  10.1 0.6 exponential_multiply_fusion.18
  10.7 0.3 copy-done.1
  11.0 0.6 convolution_bitcast_fusion.12
  11.6 0.6 convolution_bitcast_fusion.11
  12.1 0.7 pad_maximum_fusion
  12.8 0.0 all-reduce.2.cloned.1.call-update
  12.9 15.0 %all_gather.6 = f32[8,2048]{1,0:T(8,128)S(1)} all-gather(f32[8,512]{1,0:T(8,128)S(1)} %convert_multiply_fusion), channel_id=1, replica_groups=mesh['rows'=8,'cols'=4] {'cols'}, dimensions={1}, use_global_device_ids=true | all-gather | bytes 81920 | tf_op jit(solution)/shard_map/all_gather | solution.py:29
  27.9 0.0 copy-start
  28.0 0.8 %copy-done = f32[128,128]{1,0:T(8,128)S(1)} copy-done((f32[128,128]{1,0:T(8,128)S(1)}, f32[128,128]{1,0:T(8,128)}, u32[]{:S(2)}) %copy-start) | copy-done | bytes 65560
  28.8 0.1 copy.7
  28.9 14.7 %all_gather.7 = bf16[64,2048]{1,0:T(8,128)(2,1)S(1)} all-gather(bf16[64,512]{1,0:T(8,128)(2,1)S(1)} %convert_element_type.32), channel_id=1, replica_groups=mesh['rows'=8,'cols'=4] {'cols'}, dimensions={1}, use_global_device_ids=true | all-gather | bytes 327680 | tf_op jit(solution)/shard_map/all_gather | solution.py:30
  43.5 1.1 %convolution_bitcast_fusion.1 = f32[1,64,512]{2,1,0:T(8,128)S(1)} fusion(f32[]{:T(128)} %bitcast.196, f32[512]{0:T(512)S(1)} %bitcast.393, f32[512]{0:T(512)S(1)} %bitcast.395, f32[512]{0:T(512)S(1)} %bitcast.397, f32[512]{0:T(512)S(1)} %bitcast.399, f32[512]{0:T(512)S(1)} %bitcast.401, f32[512]{0:T(512)S(1)} %bitcast.403, f32[512]{0:T(512)S(1)} %bitcast.405, ...), kind=kOutput, calls=%fused_computation.1 | convolution fusion | flops 40370176 | bytes 229380 | tf_op jit(solution)/shard_map/dot_general | solution.py:41
  44.7 1.2 %convolution_bitcast_fusion = f32[1,64,512]{2,1,0:T(8,128)S(1)} fusion(f32[]{:T(128)} %bitcast.195, f32[512]{0:T(512)S(1)} %bitcast.394, f32[512]{0:T(512)S(1)} %bitcast.396, f32[512]{0:T(512)S(1)} %bitcast.398, f32[512]{0:T(512)S(1)} %bitcast.400, f32[512]{0:T(512)S(1)} %bitcast.402, f32[512]{0:T(512)S(1)} %bitcast.404, f32[512]{0:T(512)S(1)} %bitcast.406, ...), kind=kOutput, calls=%fused_computation | convolution fusion | flops 40632320 | bytes 229380 | tf_op jit(solution)/shard_map/dot_general | solution.py:42
  45.9 1.1 %convolution_bitcast_fusion.3 = f32[1,64,512]{2,1,0:T(8,128)S(1)} fusion(f32[]{:T(128)} %bitcast.197, f32[512]{0:T(512)S(1)} %bitcast.375, f32[512]{0:T(512)S(1)} %bitcast.377, f32[512]{0:T(512)S(1)} %bitcast.379, f32[512]{0:T(512)S(1)} %bitcast.381, f32[512]{0:T(512)S(1)} %bitcast.383, f32[512]{0:T(512)S(1)} %bitcast.385, f32[512]{0:T(512)S(1)} %bitcast.387, ...), kind=kOutput, calls=%fused_computation.3 | convolution fusion | flops 40370176 | bytes 229380 | tf_op jit(solution)/shard_map/dot_general | solution.py:41
  47.1 1.2 %convolution_bitcast_fusion.2 = f32[1,64,512]{2,1,0:T(8,128)S(1)} fusion(f32[]{:T(128)} %bitcast.194, f32[512]{0:T(512)S(1)} %bitcast.376, f32[512]{0:T(512)S(1)} %bitcast.378, f32[512]{0:T(512)S(1)} %bitcast.380, f32[512]{0:T(512)S(1)} %bitcast.382, f32[512]{0:T(512)S(1)} %bitcast.384, f32[512]{0:T(512)S(1)} %bitcast.386, f32[512]{0:T(512)S(1)} %bitcast.388, ...), kind=kOutput, calls=%fused_computation.2 | convolution fusion | flops 40632320 | bytes 229380 | tf_op jit(solution)/shard_map/dot_general | solution.py:42
  48.3 1.1 %convolution_bitcast_fusion.5 = f32[1,64,512]{2,1,0:T(8,128)S(1)} fusion(f32[]{:T(128)} %bitcast.198, f32[512]{0:T(512)S(1)} %bitcast.369, f32[512]{0:T(512)S(1)} %bitcast.371, f32[512]{0:T(512)S(1)} %bitcast.373, f32[512]{0:T(512)S(1)} %bitcast.425, f32[512]{0:T(512)S(1)} %bitcast.427, f32[512]{0:T(512)S(1)} %bitcast.429, f32[512]{0:T(512)S(1)} %bitcast.431, ...), kind=kOutput, calls=%fused_computation.5 | convolution fusion | flops 40370176 | bytes 229380 | tf_op jit(solution)/shard_map/dot_general | solution.py:41
  49.4 1.2 %convolution_bitcast_fusion.4 = f32[1,64,512]{2,1,0:T(8,128)S(1)} fusion(f32[]{:T(128)} %bitcast.193, f32[512]{0:T(512)S(1)} %bitcast.370, f32[512]{0:T(512)S(1)} %bitcast.372, f32[512]{0:T(512)S(1)} %bitcast.374, f32[512]{0:T(512)S(1)} %bitcast.426, f32[512]{0:T(512)S(1)} %bitcast.428, f32[512]{0:T(512)S(1)} %bitcast.430, f32[512]{0:T(512)S(1)} %bitcast.432, ...), kind=kOutput, calls=%fused_computation.4 | convolution fusion | flops 40632320 | bytes 229380 | tf_op jit(solution)/shard_map/dot_general | solution.py:42
  50.6 1.1 %convolution_bitcast_fusion.7 = f32[1,64,512]{2,1,0:T(8,128)S(1)} fusion(f32[]{:T(128)} %bitcast.189, f32[512]{0:T(512)S(1)} %bitcast.238, f32[512]{0:T(512)S(1)} %bitcast.407, f32[512]{0:T(512)S(1)} %bitcast.258, f32[512]{0:T(512)S(1)} %bitcast.409, f32[512]{0:T(512)S(1)} %bitcast.278, f32[512]{0:T(512)S(1)} %bitcast.411, f32[512]{0:T(512)S(1)} %bitcast.298, ...), kind=kOutput, calls=%fused_computation.7 | convolution fusion | flops 40370176 | bytes 229380 | tf_op jit(solution)/shard_map/dot_general | solution.py:41
  51.8 0.0 all-reduce.2.cloned.1.call-done
  51.8 0.1 collective-permute-start
  51.9 1.2 %convolution_bitcast_fusion.6 = f32[1,64,512]{2,1,0:T(8,128)S(1)} fusion(f32[]{:T(128)} %bitcast.192, f32[512]{0:T(512)S(1)} %bitcast.239, f32[512]{0:T(512)S(1)} %bitcast.408, f32[512]{0:T(512)S(1)} %bitcast.259, f32[512]{0:T(512)S(1)} %bitcast.410, f32[512]{0:T(512)S(1)} %bitcast.279, f32[512]{0:T(512)S(1)} %bitcast.412, f32[512]{0:T(512)S(1)} %bitcast.299, ...), kind=kOutput, calls=%fused_computation.6 | convolution fusion | flops 40632320 | bytes 229380 | tf_op jit(solution)/shard_map/dot_general | solution.py:42
  53.1 0.4 collective-permute-done
  53.6 1.3 %collective-permute-start.1 = (f32[2,2,64,128]{3,2,0,1:T(8,128)S(1)}, f32[2,2,64,128]{3,2,0,1:T(8,128)S(1)}, u32[]{:S(2)}, u32[]{:S(2)}) collective-permute-start(f32[2,2,64,128]{3,2,0,1:T(8,128)S(1)} %slice_add_fusion), channel_id=1, source_target_pairs={{0,8},{4,12},{8,0},{12,4},{16,24},{20,28},{24,16},{28,20},{1,9},{5... | collective-permute-start | bytes 393224 | tf_op jit(solution)/shard_map/ppermute | solution.py:8
  54.9 0.2 fusion.84
  55.1 1.0 %fusion.46 = f32[64,512]{1,0:T(8,128)S(1)} fusion(f32[64,128]{1,0:T(8,128)S(1)} %fusion.84, f32[]{:T(128)} %bitcast.199, f32[128]{0:T(128)S(1)} %get-tuple-element.81, f32[512]{0:T(512)S(1)} %bitcast.240, f32[128]{0:T(128)S(1)} %get-tuple-element.82, f32[512]{0:T(512)S(1)} %bitcast.260, f32[128]{0:T(128)S(1)} %get-tuple-element.83, f32[512]{0:T(512)S(1)} %bitcast.280, ...), kind=kOutput, calls=%fused_computation.75 | convolution fusion | flops 52035584 | bytes 184324 | tf_op jit(solution)/shard_map/dot_general | solution.py:74
  56.1 0.2 fusion.83
  56.3 1.0 %fusion.2 = f32[1,64,512]{2,1,0:T(8,128)S(1)} fusion(f32[64,512]{1,0:T(8,128)S(1)} %fusion.46, f32[64,128]{1,0:T(8,128)S(1)} %fusion.83, f32[]{:T(128)} %bitcast.200, f32[128]{0:T(128)S(1)} %get-tuple-element.81, f32[512]{0:T(512)S(1)} %bitcast.241, f32[128]{0:T(128)S(1)} %get-tuple-element.82, f32[512]{0:T(512)S(1)} %bitcast.261, ...), kind=kOutput, calls=%fused_computation.16 | convolution fusion | flops 52002816 | bytes 315396 | tf_op jit(solution)/shard_map/dot_general | solution.py:74
  57.3 1.0 %convolution_bitcast_fusion.10 = f32[1,64,512]{2,1,0:T(8,128)S(1)} fusion(f32[64,128]{1,0:T(8,128)S(1)} %fusion.84, f32[]{:T(128)} %bitcast.191, f32[128]{0:T(128)S(1)} %get-tuple-element.81, f32[512]{0:T(512)S(1)} %bitcast.242, f32[128]{0:T(128)S(1)} %get-tuple-element.82, f32[512]{0:T(512)S(1)} %bitcast.262, f32[128]{0:T(128)S(1)} %get-tuple-element.83, ...), kind=kOutput, calls=%fused_computation.10 | convolution fusion | flops 51970048 | bytes 184324 | tf_op jit(solution)/shard_map/dot_general | solution.py:73
  58.2 0.9 %collective-permute-done.1 = f32[2,2,64,128]{3,2,0,1:T(8,128)S(1)} collective-permute-done((f32[2,2,64,128]{3,2,0,1:T(8,128)S(1)}, f32[2,2,64,128]{3,2,0,1:T(8,128)S(1)}, u32[]{:S(2)}, u32[]{:S(2)}) %collective-permute-start.1) | collective-permute-done | bytes 131104 | tf_op jit(solution)/shard_map/ppermute | solution.py:8
  59.2 1.4 %collective-permute-start.2 = (f32[1,2,64,128]{3,2,0,1:T(8,128)S(1)}, f32[1,2,64,128]{3,2,0,1:T(8,128)S(1)}, u32[]{:S(2)}, u32[]{:S(2)}) collective-permute-start(f32[1,2,64,128]{3,2,0,1:T(8,128)S(1)} %slice_add_fusion.1), channel_id=1, source_target_pairs={{0,16},{4,20},{8,24},{12,28},{16,0},{20,4},{24,8},{28,12},{1,17},{... | collective-permute-start | bytes 196616 | tf_op jit(solution)/shard_map/ppermute | solution.py:8
  60.6 0.2 fusion.82
  60.7 1.2 %fusion.44 = f32[64,512]{1,0:T(8,128)S(1)} fusion(f32[64,128]{1,0:T(8,128)S(1)} %fusion.82, f32[]{:T(128)} %bitcast.201, f32[128]{0:T(128)S(1)} %get-tuple-element.110, f32[128]{0:T(128)S(1)} %get-tuple-element.109, f32[128]{0:T(128)S(1)} %get-tuple-element.108, f32[128]{0:T(128)S(1)} %get-tuple-element.107, f32[128]{0:T(128)S(1)} %get-tuple-element.106, ...), kind=kOutput, calls=%fused_computation.71 | convolution fusion | flops 52035584 | bytes 184324 | tf_op jit(solution)/shard_map/dot_general | solution.py:74
  62.0 0.2 fusion.81
  62.1 1.0 %fusion.1 = f32[1,64,512]{2,1,0:T(8,128)S(1)} fusion(f32[64,512]{1,0:T(8,128)S(1)} %fusion.44, f32[64,128]{1,0:T(8,128)S(1)} %fusion.81, f32[]{:T(128)} %bitcast.202, f32[128]{0:T(128)S(1)} %get-tuple-element.110, f32[128]{0:T(128)S(1)} %get-tuple-element.109, f32[128]{0:T(128)S(1)} %get-tuple-element.108, f32[128]{0:T(128)S(1)} %get-tuple-element.107, ...), kind=kOutput, calls=%fused_computation.14 | convolution fusion | flops 52002816 | bytes 315396 | tf_op jit(solution)/shard_map/dot_general | solution.py:74
  63.1 1.0 %convolution_bitcast_fusion.9 = f32[1,64,512]{2,1,0:T(8,128)S(1)} fusion(f32[64,128]{1,0:T(8,128)S(1)} %fusion.82, f32[]{:T(128)} %bitcast.206, f32[128]{0:T(128)S(1)} %get-tuple-element.110, f32[128]{0:T(128)S(1)} %get-tuple-element.109, f32[128]{0:T(128)S(1)} %get-tuple-element.108, f32[128]{0:T(128)S(1)} %get-tuple-element.107, ...), kind=kOutput, calls=%fused_computation.9 | convolution fusion | flops 51970048 | bytes 184324 | tf_op jit(solution)/shard_map/dot_general | solution.py:73
  64.1 0.2 fusion.80
  64.3 1.0 %convolution_bitcast_fusion.8 = f32[1,64,512]{2,1,0:T(8,128)S(1)} fusion(f32[64,128]{1,0:T(8,128)S(1)} %fusion.80, f32[]{:T(128)} %bitcast.205, f32[128]{0:T(128)S(1)} %get-tuple-element.97, f32[128]{0:T(128)S(1)} %get-tuple-element.98, f32[128]{0:T(128)S(1)} %get-tuple-element.99, f32[128]{0:T(128)S(1)} %get-tuple-element.100, ...), kind=kOutput, calls=%fused_computation.8 | convolution fusion | flops 51970048 | bytes 184324 | tf_op jit(solution)/shard_map/dot_general | solution.py:73
  65.3 1.0 %fusion.42 = f32[64,512]{1,0:T(8,128)S(1)} fusion(f32[64,128]{1,0:T(8,128)S(1)} %fusion.80, f32[]{:T(128)} %bitcast.203, f32[128]{0:T(128)S(1)} %get-tuple-element.97, f32[128]{0:T(128)S(1)} %get-tuple-element.98, f32[128]{0:T(128)S(1)} %get-tuple-element.99, f32[128]{0:T(128)S(1)} %get-tuple-element.100, f32[128]{0:T(128)S(1)} %get-tuple-element.101, ...), kind=kOutput, calls=%fused_computation.67 | convolution fusion | flops 52035584 | bytes 184324 | tf_op jit(solution)/shard_map/dot_general | solution.py:74
  66.3 0.2 fusion.79
  66.5 1.0 %fusion = f32[1,64,512]{2,1,0:T(8,128)S(1)} fusion(f32[64,512]{1,0:T(8,128)S(1)} %fusion.42, f32[64,128]{1,0:T(8,128)S(1)} %fusion.79, f32[]{:T(128)} %bitcast.204, f32[128]{0:T(128)S(1)} %get-tuple-element.97, f32[128]{0:T(128)S(1)} %get-tuple-element.98, f32[128]{0:T(128)S(1)} %get-tuple-element.99, f32[128]{0:T(128)S(1)} %get-tuple-element.100, ...), kind=kOutput, calls=%fused_computation.12 | convolution fusion | flops 52002816 | bytes 315396 | tf_op jit(solution)/shard_map/dot_general | solution.py:74
  67.5 0.9 %fusion.41 = f32[2,64,512]{2,1,0:T(8,128)} fusion(f32[1,64,512]{2,1,0:T(8,128)S(1)} %convolution_bitcast_fusion.6, f32[1,64,512]{2,1,0:T(8,128)S(1)} %convolution_bitcast_fusion.7, f32[1,64,512]{2,1,0:T(8,128)S(1)} %convolution_bitcast_fusion.4, f32[1,64,512]{2,1,0:T(8,128)S(1)} %convolution_bitcast_fusion.5, ...), kind=kLoop, calls=%fused_computation.66 | loop fusion | flops 851968 | bytes 2097152 | tf_op jit(solution)/shard_map/add | solution.py:77
  (15 shorter events, 0.1 us)
Async XLA Ops:
  6.5 0.7 copy-start.3
  6.5 45.3 %all-reduce.2.cloned.1.call-start = ((), (), s32[]{:S(2)}) async-start(), calls=%async_computation | async-start | bytes 393216 | tf_op jit(solution)/shard_map/psum | solution.py:60
  6.5 0.7 copy-start.4
  10.1 0.9 %copy-start.1 = (f32[64,512]{1,0:T(8,128)S(1)}, f32[64,512]{1,0:T(8,128)}, u32[]{:S(2)}) copy-start(f32[64,512]{1,0:T(8,128)} %param.11) | copy-start | bytes 393220
  27.9 0.8 %copy-start = (f32[128,128]{1,0:T(8,128)S(1)}, f32[128,128]{1,0:T(8,128)}, u32[]{:S(2)}) copy-start(f32[128,128]{1,0:T(8,128)} %param.15) | copy-start | bytes 196612
  51.8 1.7 %collective-permute-start = (f32[3,2,64,128]{3,2,0,1:T(8,128)}, f32[3,2,64,128]{3,2,0,1:T(8,128)S(1)}, u32[]{:S(2)}, u32[]{:S(2)}) collective-permute-start(f32[3,2,64,128]{3,2,0,1:T(8,128)} %all-reduce.2.cloned.1.call-done), channel_id=1, source_target_pairs={{0,4},{4,0},{8,12},{12,8},{16,20},{20,16},{24,28},{28,24},{1,5},{5... | collective-permute-start | bytes 589832 | tf_op jit(solution)/shard_map/ppermute | solution.py:8
  51.9 1.6 %copy-start.2 = (f32[3,2,64,128]{3,2,0,1:T(8,128)S(1)}, f32[3,2,64,128]{3,2,0,1:T(8,128)}, u32[]{:S(2)}) copy-start(f32[3,2,64,128]{3,2,0,1:T(8,128)} %all-reduce.2.cloned.1.call-done) | copy-start | bytes 589828
  53.6 5.6 %collective-permute-start.1 = (f32[2,2,64,128]{3,2,0,1:T(8,128)S(1)}, f32[2,2,64,128]{3,2,0,1:T(8,128)S(1)}, u32[]{:S(2)}, u32[]{:S(2)}) collective-permute-start(f32[2,2,64,128]{3,2,0,1:T(8,128)S(1)} %slice_add_fusion), channel_id=1, source_target_pairs={{0,8},{4,12},{8,0},{12,4},{16,24},{20,28},{24,16},{28,20},{1,9},{5... | collective-permute-start | bytes 393224 | tf_op jit(solution)/shard_map/ppermute | solution.py:8
  59.2 4.9 %collective-permute-start.2 = (f32[1,2,64,128]{3,2,0,1:T(8,128)S(1)}, f32[1,2,64,128]{3,2,0,1:T(8,128)S(1)}, u32[]{:S(2)}, u32[]{:S(2)}) collective-permute-start(f32[1,2,64,128]{3,2,0,1:T(8,128)S(1)} %slice_add_fusion.1), channel_id=1, source_target_pairs={{0,16},{4,20},{8,24},{12,28},{16,0},{20,4},{24,8},{28,12},{1,17},{... | collective-permute-start | bytes 196616 | tf_op jit(solution)/shard_map/ppermute | solution.py:8
Sparse Core Ops, SparseCore 0:
  13.0 38.0 all-reduce.1
where the time goes:
time: 75.5 us; the launch traced here: 75.2 us
  blocking collectives  29.7 us (39%)
  matrix products  20.8 us (28%)
  between operations  14.3 us (19%)
  other arithmetic  4.35 us (6%)
  starting transfers between devices  2.77 us (4%)
  local copies, waits for them, and re-layouts  1.91 us (3%)
  waiting for transfers between devices  1.38 us (2%)
    all_gather x1, blocking collectives, on_device(): leaf_points = lax.all_gather(scaled, 'cols', axis=1, tiled=True)  15 us
    all_gather x1, blocking collectives, on_device(): leaf_signs = lax.all_gather(signs_half, 'cols', axis=1, tiled=True)  14.7 us
    dot_general x4, matrix products, on_device(): jnp.dot(block_signs, slope_half, preferred_element_type=jnp.float32)  4.86 us
    dot_general x4, matrix products, on_device(): jnp.dot(block_signs, kernel_half, preferred_element_type=jnp.float32)  4.57 us
    dot_general x3, matrix products, on_device(): jnp.dot(first, dfactor_stack[level].T, precision=highest)  3.17 us
    dot_general x3, matrix products, on_device(): jnp.dot(second, factor_stack[level].T, precision=highest)  2.95 us
    dot_general x3, matrix products, on_device(): value = jnp.dot(first, factor_stack[level].T, precision=highest)  2.95 us
    ppermute x3, starting transfers between devices, swapped(): lax.ppermute(array, axis, [(i, i ^ 1 << apart) for i in range(lax.axis_si...  2.77 us
  transfers between devices with their start and end apart: 4, of which 2 were waited for; matrix products, arithmetic and copies ran while one was open for 22% of the time, Pallas kernels for 0%

commit v1 on v0

--- a/solution.py
+++ b/solution.py
@@ -26,8 +26,11 @@
     groups = lax.axis_size("cols")
     rows_index = lax.axis_index("rows")
     levels = lax.axis_size("rows").bit_length() - 1
-    leaf_points = lax.all_gather(scaled, "cols", axis=1, tiled=True)
-    leaf_signs = lax.all_gather(signs_half, "cols", axis=1, tiled=True)
+    leaf_points, leaf_signs = jnp.split(
+        lax.all_gather(jnp.concatenate([scaled, signs_half], axis=0), "cols", axis=1, tiled=True),
+        [scaled.shape[0]],
+        axis=0,
+    )
     accumulated = jnp.zeros((2, probes.shape[0], width), jnp.float32)
     for row_block in range(groups):
         block_points = leaf_points[:, row_block * width : (row_block + 1) * width]

time: 75.5 us -> 75.7 us (level)
  blocking collectives: 29.7 us -> 21.7 us
  waiting for transfers between devices: 1.38 us -> 9.34 us
    psum x1, waiting for transfers between devices: 0.02 us -> 8.15 us  [on_device(): lax.psum(jnp.stack([own_project, own_dproject], axis=1), 'cols')]
    all_gather x2 -> x1, blocking collectives: 29.7 us -> 21.7 us  [on_device(): lax.all_gather(jnp.concatenate([scaled, signs_half], axis=0), 'cols', axi...]
  transfers between devices with their start and end apart: 4 -> 4, of which waited for: 2 -> 3; matrix products, arithmetic and copies ran while one was open for 22% -> 22% of each run, Pallas kernels for 0% -> 0%
where the time goes in v1:
time: 75.7 us; the launch traced here: 75.4 us
  blocking collectives  21.7 us (29%)
  matrix products  20.8 us (27%)
  between operations  14.3 us (19%)
  waiting for transfers between devices  9.34 us (12%)
  other arithmetic  4.37 us (6%)
  starting transfers between devices  2.99 us (4%)
  local copies, waits for them, and re-layouts  1.93 us (3%)
    all_gather x1, blocking collectives, on_device(): lax.all_gather(jnp.concatenate([scaled, signs_half], axis=0), 'cols', axi...  21.7 us
    psum x1, waiting for transfers between devices, on_device(): lax.psum(jnp.stack([own_project, own_dproject], axis=1), 'cols')  8.15 us
    dot_general x4, matrix products, on_device(): jnp.dot(block_signs, slope_half, preferred_element_type=jnp.float32)  4.86 us
    dot_general x4, matrix products, on_device(): jnp.dot(block_signs, kernel_half, preferred_element_type=jnp.float32)  4.57 us
    dot_general x3, matrix products, on_device(): jnp.dot(first, dfactor_stack[level].T, precision=highest)  3.17 us
    ppermute x3, starting transfers between devices, swapped(): lax.ppermute(array, axis, [(i, i ^ 1 << apart) for i in range(lax.axis_si...  2.99 us
    dot_general x3, matrix products, on_device(): jnp.dot(second, factor_stack[level].T, precision=highest)  2.95 us
    dot_general x3, matrix products, on_device(): value = jnp.dot(first, factor_stack[level].T, precision=highest)  2.95 us
  transfers between devices with their start and end apart: 4, of which 3 were waited for; matrix products, arithmetic and copies ran while one was open for 22% of the time, Pallas kernels for 0%

profile of v1, /device:TPU:0, one launch (start us, length us, event | category | flops | bytes accessed | tf_op | source)
XLA Modules:
  0.0 75.4 jit_solution(4288899651698319164)
XLA Ops:
  6.5 0.0 all-reduce.2.cloned.1.call-start
  6.5 0.7 copy-done.4
  7.2 0.0 copy-done.3
  7.3 0.1 convert_multiply_fusion
  8.0 0.8 %bitcast_multiply_fusion.2 = (f32[8,128]{1,0:T(8,128)S(1)}, f32[8,128]{1,0:T(8,128)S(1)}, f32[8,128]{1,0:T(8,128)S(1)}) fusion(f32[14,8,128]{2,1,0:T(8,128)} %param.14, s32[]{:T(128)S(6)} %select_n.30, f32[8]{0:T(128)S(1)} %get-tuple-element.30, s32[]{:T(128)S(6)} %select_n.32, s32[]{:T(128)S(6)} %select_n.31), kind=kLoop, calls=%fused_computation.139 | loop fusion | flops 3072 | bytes 24620 | tf_op jit(solution)/shard_map/mul | solution.py:55
  8.8 0.6 exponential_multiply_fusion.17
  9.4 0.6 exponential_multiply_fusion.16
  10.1 0.0 copy-start.1
  10.1 0.6 exponential_multiply_fusion.18
  10.7 0.3 copy-done.1
  11.0 0.6 convolution_bitcast_fusion.12
  11.6 0.6 convolution_bitcast_fusion.11
  12.1 0.7 pad_maximum_fusion
  12.8 0.0 all-reduce.2.cloned.1.call-update
  12.9 21.7 %all_gather.3 = f32[72,2048]{1,0:T(8,128)S(1)} all-gather(f32[72,512]{1,0:T(8,128)S(1)} %pad_maximum_fusion.1), channel_id=1, replica_groups=mesh['rows'=8,'cols'=4] {'cols'}, dimensions={1}, use_global_device_ids=true | all-gather | bytes 737280 | tf_op jit(solution)/shard_map/all_gather | solution.py:30
  34.6 0.8 %copy-done = f32[128,128]{1,0:T(8,128)S(1)} copy-done((f32[128,128]{1,0:T(8,128)S(1)}, f32[128,128]{1,0:T(8,128)}, u32[]{:S(2)}) %copy-start) | copy-done | bytes 65560
  35.4 0.1 copy.7
  35.5 1.1 %convolution_bitcast_fusion.1 = f32[1,64,512]{2,1,0:T(8,128)S(1)} fusion(f32[]{:T(128)} %bitcast.180, f32[512]{0:T(512)S(1)} %bitcast.377, f32[512]{0:T(512)S(1)} %bitcast.379, f32[512]{0:T(512)S(1)} %bitcast.381, f32[512]{0:T(512)S(1)} %bitcast.383, f32[512]{0:T(512)S(1)} %bitcast.385, f32[512]{0:T(512)S(1)} %bitcast.387, f32[512]{0:T(512)S(1)} %bitcast.389, ...), kind=kOutput, calls=%fused_computation.1 | convolution fusion | flops 40370176 | bytes 229380 | tf_op jit(solution)/shard_map/dot_general | solution.py:44
  36.7 1.2 %convolution_bitcast_fusion = f32[1,64,512]{2,1,0:T(8,128)S(1)} fusion(f32[]{:T(128)} %bitcast.179, f32[512]{0:T(512)S(1)} %bitcast.378, f32[512]{0:T(512)S(1)} %bitcast.380, f32[512]{0:T(512)S(1)} %bitcast.382, f32[512]{0:T(512)S(1)} %bitcast.384, f32[512]{0:T(512)S(1)} %bitcast.386, f32[512]{0:T(512)S(1)} %bitcast.388, f32[512]{0:T(512)S(1)} %bitcast.390, ...), kind=kOutput, calls=%fused_computation | convolution fusion | flops 40632320 | bytes 229380 | tf_op jit(solution)/shard_map/dot_general | solution.py:45
  37.9 1.1 %convolution_bitcast_fusion.3 = f32[1,64,512]{2,1,0:T(8,128)S(1)} fusion(f32[]{:T(128)} %bitcast.181, f32[512]{0:T(512)S(1)} %bitcast.359, f32[512]{0:T(512)S(1)} %bitcast.361, f32[512]{0:T(512)S(1)} %bitcast.363, f32[512]{0:T(512)S(1)} %bitcast.365, f32[512]{0:T(512)S(1)} %bitcast.367, f32[512]{0:T(512)S(1)} %bitcast.369, f32[512]{0:T(512)S(1)} %bitcast.371, ...), kind=kOutput, calls=%fused_computation.3 | convolution fusion | flops 40370176 | bytes 229380 | tf_op jit(solution)/shard_map/dot_general | solution.py:44
  39.1 1.2 %convolution_bitcast_fusion.2 = f32[1,64,512]{2,1,0:T(8,128)S(1)} fusion(f32[]{:T(128)} %bitcast.178, f32[512]{0:T(512)S(1)} %bitcast.360, f32[512]{0:T(512)S(1)} %bitcast.362, f32[512]{0:T(512)S(1)} %bitcast.364, f32[512]{0:T(512)S(1)} %bitcast.366, f32[512]{0:T(512)S(1)} %bitcast.368, f32[512]{0:T(512)S(1)} %bitcast.370, f32[512]{0:T(512)S(1)} %bitcast.372, ...), kind=kOutput, calls=%fused_computation.2 | convolution fusion | flops 40632320 | bytes 229380 | tf_op jit(solution)/shard_map/dot_general | solution.py:45
  40.3 1.1 %convolution_bitcast_fusion.5 = f32[1,64,512]{2,1,0:T(8,128)S(1)} fusion(f32[]{:T(128)} %bitcast.182, f32[512]{0:T(512)S(1)} %bitcast.353, f32[512]{0:T(512)S(1)} %bitcast.355, f32[512]{0:T(512)S(1)} %bitcast.357, f32[512]{0:T(512)S(1)} %bitcast.409, f32[512]{0:T(512)S(1)} %bitcast.411, f32[512]{0:T(512)S(1)} %bitcast.413, f32[512]{0:T(512)S(1)} %bitcast.415, ...), kind=kOutput, calls=%fused_computation.5 | convolution fusion | flops 40370176 | bytes 229380 | tf_op jit(solution)/shard_map/dot_general | solution.py:44
  41.4 1.2 %convolution_bitcast_fusion.4 = f32[1,64,512]{2,1,0:T(8,128)S(1)} fusion(f32[]{:T(128)} %bitcast.177, f32[512]{0:T(512)S(1)} %bitcast.354, f32[512]{0:T(512)S(1)} %bitcast.356, f32[512]{0:T(512)S(1)} %bitcast.358, f32[512]{0:T(512)S(1)} %bitcast.410, f32[512]{0:T(512)S(1)} %bitcast.412, f32[512]{0:T(512)S(1)} %bitcast.414, f32[512]{0:T(512)S(1)} %bitcast.416, ...), kind=kOutput, calls=%fused_computation.4 | convolution fusion | flops 40632320 | bytes 229380 | tf_op jit(solution)/shard_map/dot_general | solution.py:45
  42.7 1.1 %convolution_bitcast_fusion.7 = f32[1,64,512]{2,1,0:T(8,128)S(1)} fusion(f32[]{:T(128)} %bitcast.173, f32[512]{0:T(512)S(1)} %bitcast.222, f32[512]{0:T(512)S(1)} %bitcast.391, f32[512]{0:T(512)S(1)} %bitcast.242, f32[512]{0:T(512)S(1)} %bitcast.393, f32[512]{0:T(512)S(1)} %bitcast.262, f32[512]{0:T(512)S(1)} %bitcast.395, f32[512]{0:T(512)S(1)} %bitcast.282, ...), kind=kOutput, calls=%fused_computation.7 | convolution fusion | flops 40370176 | bytes 229380 | tf_op jit(solution)/shard_map/dot_general | solution.py:44
  43.8 8.1 %all-reduce.2.cloned.1.call-done = f32[3,2,64,128]{3,2,0,1:T(8,128)} async-done(((f32[3,2,64,128]{3,2,0,1:T(8,128)}), f32[3,2,64,128]{3,2,0,1:T(8,128)}) %all-reduce.2.cloned.1.call-update) | async-done | bytes 196624 | tf_op jit(solution)/shard_map/psum | solution.py:63
  52.0 0.0 collective-permute-start
  52.0 1.2 %convolution_bitcast_fusion.6 = f32[1,64,512]{2,1,0:T(8,128)S(1)} fusion(f32[]{:T(128)} %bitcast.176, f32[512]{0:T(512)S(1)} %bitcast.223, f32[512]{0:T(512)S(1)} %bitcast.392, f32[512]{0:T(512)S(1)} %bitcast.243, f32[512]{0:T(512)S(1)} %bitcast.394, f32[512]{0:T(512)S(1)} %bitcast.263, f32[512]{0:T(512)S(1)} %bitcast.396, f32[512]{0:T(512)S(1)} %bitcast.283, ...), kind=kOutput, calls=%fused_computation.6 | convolution fusion | flops 40632320 | bytes 229380 | tf_op jit(solution)/shard_map/dot_general | solution.py:45
  53.2 0.4 collective-permute-done
  53.6 1.5 %collective-permute-start.1 = (f32[2,2,64,128]{3,2,0,1:T(8,128)S(1)}, f32[2,2,64,128]{3,2,0,1:T(8,128)S(1)}, u32[]{:S(2)}, u32[]{:S(2)}) collective-permute-start(f32[2,2,64,128]{3,2,0,1:T(8,128)S(1)} %slice_add_fusion), channel_id=1, source_target_pairs={{0,8},{4,12},{8,0},{12,4},{16,24},{20,28},{24,16},{28,20},{1,9},{5... | collective-permute-start | bytes 393224 | tf_op jit(solution)/shard_map/ppermute | solution.py:8
  55.1 0.2 fusion.84
  55.3 1.0 %fusion.46 = f32[64,512]{1,0:T(8,128)S(1)} fusion(f32[64,128]{1,0:T(8,128)S(1)} %fusion.84, f32[]{:T(128)} %bitcast.183, f32[128]{0:T(128)S(1)} %get-tuple-element.81, f32[512]{0:T(512)S(1)} %bitcast.224, f32[128]{0:T(128)S(1)} %get-tuple-element.82, f32[512]{0:T(512)S(1)} %bitcast.244, f32[128]{0:T(128)S(1)} %get-tuple-element.83, f32[512]{0:T(512)S(1)} %bitcast.264, ...), kind=kOutput, calls=%fused_computation.75 | convolution fusion | flops 52035584 | bytes 184324 | tf_op jit(solution)/shard_map/dot_general | solution.py:77
  56.3 0.2 fusion.83
  56.5 1.0 %fusion.2 = f32[1,64,512]{2,1,0:T(8,128)S(1)} fusion(f32[64,512]{1,0:T(8,128)S(1)} %fusion.46, f32[64,128]{1,0:T(8,128)S(1)} %fusion.83, f32[]{:T(128)} %bitcast.184, f32[128]{0:T(128)S(1)} %get-tuple-element.81, f32[512]{0:T(512)S(1)} %bitcast.225, f32[128]{0:T(128)S(1)} %get-tuple-element.82, f32[512]{0:T(512)S(1)} %bitcast.245, ...), kind=kOutput, calls=%fused_computation.16 | convolution fusion | flops 52002816 | bytes 315396 | tf_op jit(solution)/shard_map/dot_general | solution.py:77
  57.5 1.0 %convolution_bitcast_fusion.10 = f32[1,64,512]{2,1,0:T(8,128)S(1)} fusion(f32[64,128]{1,0:T(8,128)S(1)} %fusion.84, f32[]{:T(128)} %bitcast.175, f32[128]{0:T(128)S(1)} %get-tuple-element.81, f32[512]{0:T(512)S(1)} %bitcast.226, f32[128]{0:T(128)S(1)} %get-tuple-element.82, f32[512]{0:T(512)S(1)} %bitcast.246, f32[128]{0:T(128)S(1)} %get-tuple-element.83, ...), kind=kOutput, calls=%fused_computation.10 | convolution fusion | flops 51970048 | bytes 184324 | tf_op jit(solution)/shard_map/dot_general | solution.py:76
  58.5 0.7 collective-permute-done.1
  59.2 1.5 %collective-permute-start.2 = (f32[1,2,64,128]{3,2,0,1:T(8,128)S(1)}, f32[1,2,64,128]{3,2,0,1:T(8,128)S(1)}, u32[]{:S(2)}, u32[]{:S(2)}) collective-permute-start(f32[1,2,64,128]{3,2,0,1:T(8,128)S(1)} %slice_add_fusion.1), channel_id=1, source_target_pairs={{0,16},{4,20},{8,24},{12,28},{16,0},{20,4},{24,8},{28,12},{1,17},{... | collective-permute-start | bytes 196616 | tf_op jit(solution)/shard_map/ppermute | solution.py:8
  60.7 0.2 fusion.82
  60.9 1.2 %fusion.44 = f32[64,512]{1,0:T(8,128)S(1)} fusion(f32[64,128]{1,0:T(8,128)S(1)} %fusion.82, f32[]{:T(128)} %bitcast.185, f32[128]{0:T(128)S(1)} %get-tuple-element.110, f32[128]{0:T(128)S(1)} %get-tuple-element.109, f32[128]{0:T(128)S(1)} %get-tuple-element.108, f32[128]{0:T(128)S(1)} %get-tuple-element.107, f32[128]{0:T(128)S(1)} %get-tuple-element.106, ...), kind=kOutput, calls=%fused_computation.71 | convolution fusion | flops 52035584 | bytes 184324 | tf_op jit(solution)/shard_map/dot_general | solution.py:77
  62.1 0.2 fusion.81
  62.3 1.0 %fusion.1 = f32[1,64,512]{2,1,0:T(8,128)S(1)} fusion(f32[64,512]{1,0:T(8,128)S(1)} %fusion.44, f32[64,128]{1,0:T(8,128)S(1)} %fusion.81, f32[]{:T(128)} %bitcast.186, f32[128]{0:T(128)S(1)} %get-tuple-element.110, f32[128]{0:T(128)S(1)} %get-tuple-element.109, f32[128]{0:T(128)S(1)} %get-tuple-element.108, f32[128]{0:T(128)S(1)} %get-tuple-element.107, ...), kind=kOutput, calls=%fused_computation.14 | convolution fusion | flops 52002816 | bytes 315396 | tf_op jit(solution)/shard_map/dot_general | solution.py:77
  63.3 1.0 %convolution_bitcast_fusion.9 = f32[1,64,512]{2,1,0:T(8,128)S(1)} fusion(f32[64,128]{1,0:T(8,128)S(1)} %fusion.82, f32[]{:T(128)} %bitcast.190, f32[128]{0:T(128)S(1)} %get-tuple-element.110, f32[128]{0:T(128)S(1)} %get-tuple-element.109, f32[128]{0:T(128)S(1)} %get-tuple-element.108, f32[128]{0:T(128)S(1)} %get-tuple-element.107, ...), kind=kOutput, calls=%fused_computation.9 | convolution fusion | flops 51970048 | bytes 184324 | tf_op jit(solution)/shard_map/dot_general | solution.py:76
  64.3 0.0 collective-permute-done.2
  64.3 0.2 fusion.80
  64.5 1.0 %convolution_bitcast_fusion.8 = f32[1,64,512]{2,1,0:T(8,128)S(1)} fusion(f32[64,128]{1,0:T(8,128)S(1)} %fusion.80, f32[]{:T(128)} %bitcast.189, f32[128]{0:T(128)S(1)} %get-tuple-element.97, f32[128]{0:T(128)S(1)} %get-tuple-element.98, f32[128]{0:T(128)S(1)} %get-tuple-element.99, f32[128]{0:T(128)S(1)} %get-tuple-element.100, ...), kind=kOutput, calls=%fused_computation.8 | convolution fusion | flops 51970048 | bytes 184324 | tf_op jit(solution)/shard_map/dot_general | solution.py:76
  65.5 1.0 %fusion.42 = f32[64,512]{1,0:T(8,128)S(1)} fusion(f32[64,128]{1,0:T(8,128)S(1)} %fusion.80, f32[]{:T(128)} %bitcast.187, f32[128]{0:T(128)S(1)} %get-tuple-element.97, f32[128]{0:T(128)S(1)} %get-tuple-element.98, f32[128]{0:T(128)S(1)} %get-tuple-element.99, f32[128]{0:T(128)S(1)} %get-tuple-element.100, f32[128]{0:T(128)S(1)} %get-tuple-element.101, ...), kind=kOutput, calls=%fused_computation.67 | convolution fusion | flops 52035584 | bytes 184324 | tf_op jit(solution)/shard_map/dot_general | solution.py:77
  66.4 0.2 fusion.79
  66.6 1.0 %fusion = f32[1,64,512]{2,1,0:T(8,128)S(1)} fusion(f32[64,512]{1,0:T(8,128)S(1)} %fusion.42, f32[64,128]{1,0:T(8,128)S(1)} %fusion.79, f32[]{:T(128)} %bitcast.188, f32[128]{0:T(128)S(1)} %get-tuple-element.97, f32[128]{0:T(128)S(1)} %get-tuple-element.98, f32[128]{0:T(128)S(1)} %get-tuple-element.99, f32[128]{0:T(128)S(1)} %get-tuple-element.100, ...), kind=kOutput, calls=%fused_computation.12 | convolution fusion | flops 52002816 | bytes 315396 | tf_op jit(solution)/shard_map/dot_general | solution.py:77
  67.6 0.9 %fusion.41 = f32[2,64,512]{2,1,0:T(8,128)} fusion(f32[1,64,512]{2,1,0:T(8,128)S(1)} %convolution_bitcast_fusion.6, f32[1,64,512]{2,1,0:T(8,128)S(1)} %convolution_bitcast_fusion.7, f32[1,64,512]{2,1,0:T(8,128)S(1)} %convolution_bitcast_fusion.4, f32[1,64,512]{2,1,0:T(8,128)S(1)} %convolution_bitcast_fusion.5, ...), kind=kLoop, calls=%fused_computation.66 | loop fusion | flops 851968 | bytes 2097152 | tf_op jit(solution)/shard_map/add | solution.py:80
  (15 shorter events, 0.1 us)
Async XLA Ops:
  6.5 0.7 copy-start.3
  6.5 45.4 %all-reduce.2.cloned.1.call-start = ((), (), s32[]{:S(2)}) async-start(), calls=%async_computation | async-start | bytes 393216 | tf_op jit(solution)/shard_map/psum | solution.py:63
  6.5 0.7 copy-start.4
  10.1 0.9 %copy-start.1 = (f32[64,512]{1,0:T(8,128)S(1)}, f32[64,512]{1,0:T(8,128)}, u32[]{:S(2)}) copy-start(f32[64,512]{1,0:T(8,128)} %param.11) | copy-start | bytes 393220
  34.6 0.8 %copy-start = (f32[128,128]{1,0:T(8,128)S(1)}, f32[128,128]{1,0:T(8,128)}, u32[]{:S(2)}) copy-start(f32[128,128]{1,0:T(8,128)} %param.15) | copy-start | bytes 196612
  52.0 1.7 %collective-permute-start = (f32[3,2,64,128]{3,2,0,1:T(8,128)}, f32[3,2,64,128]{3,2,0,1:T(8,128)S(1)}, u32[]{:S(2)}, u32[]{:S(2)}) collective-permute-start(f32[3,2,64,128]{3,2,0,1:T(8,128)} %all-reduce.2.cloned.1.call-done), channel_id=1, source_target_pairs={{0,4},{4,0},{8,12},{12,8},{16,20},{20,16},{24,28},{28,24},{1,5},{5... | collective-permute-start | bytes 589832 | tf_op jit(solution)/shard_map/ppermute | solution.py:8
  52.0 1.7 %copy-start.2 = (f32[3,2,64,128]{3,2,0,1:T(8,128)S(1)}, f32[3,2,64,128]{3,2,0,1:T(8,128)}, u32[]{:S(2)}) copy-start(f32[3,2,64,128]{3,2,0,1:T(8,128)} %all-reduce.2.cloned.1.call-done) | copy-start | bytes 589828
  53.6 5.6 %collective-permute-start.1 = (f32[2,2,64,128]{3,2,0,1:T(8,128)S(1)}, f32[2,2,64,128]{3,2,0,1:T(8,128)S(1)}, u32[]{:S(2)}, u32[]{:S(2)}) collective-permute-start(f32[2,2,64,128]{3,2,0,1:T(8,128)S(1)} %slice_add_fusion), channel_id=1, source_target_pairs={{0,8},{4,12},{8,0},{12,4},{16,24},{20,28},{24,16},{28,20},{1,9},{5... | collective-permute-start | bytes 393224 | tf_op jit(solution)/shard_map/ppermute | solution.py:8
  59.2 5.0 %collective-permute-start.2 = (f32[1,2,64,128]{3,2,0,1:T(8,128)S(1)}, f32[1,2,64,128]{3,2,0,1:T(8,128)S(1)}, u32[]{:S(2)}, u32[]{:S(2)}) collective-permute-start(f32[1,2,64,128]{3,2,0,1:T(8,128)S(1)} %slice_add_fusion.1), channel_id=1, source_target_pairs={{0,16},{4,20},{8,24},{12,28},{16,0},{20,4},{24,8},{28,12},{1,17},{... | collective-permute-start | bytes 196616 | tf_op jit(solution)/shard_map/ppermute | solution.py:8
Sparse Core Ops, SparseCore 0:
  13.0 38.9 all-reduce.1
